TPU v7x, 32 devices: a whole 2x2x4 slice. The times are simulated.
32 devices in a mesh: dp: 2 (over core), mp: 16 (over z, y, x).
Axes of the slice: x: 2, y: 2, z: 4, core: 2. Of those that a mesh axis runs over, the one named last changes fastest.
Arguments:
- inputs: bfloat16 [512, 4096], P('dp'), may hold values from -6 to 6
- upstream: bfloat16 [512, 4096], P('dp'), may hold values from -6 to 6
- eig_tiles: bfloat16 [16, 8, 8, 128, 128], P('mp'), may hold values from -0.09375 to 0.09375
- eigvals: float32 [4096], replicated, may hold values from 0.25 to 4
Outputs:
- grad_t: bfloat16 [4096, 512], P('mp', 'dp')
All inputs are finite; a program needn't handle non-finite values.
Results may differ from a plain program's by a relative error of at most 0.013.
Values may be sent and summed in bfloat16 or wider, within the bound.
A program may use at most 64 MiB of HBM per device.

v0:
```python
import jax
import jax.numpy as jnp
from jax import lax
from jax.sharding import PartitionSpec as P


def kernel_of(left, right):
    root_left = jnp.sqrt(left)[:, None]
    root_right = jnp.sqrt(right)[None, :]
    return -1.0 / (root_left * root_right * (root_left + root_right))


def on_device(inputs, upstream, eig_tiles, eigvals):
    groups = lax.axis_size("mp")
    member = lax.axis_index("mp")
    width = eigvals.shape[0]
    slab = width // groups
    tile_rows = eig_tiles.shape[1]
    tile_cols = eig_tiles.shape[2]
    tile = eig_tiles.shape[3]
    grid_rows = width // (tile_rows * tile)
    grid_cols = groups // grid_rows
    piece = tile_cols * tile // groups
    local = jnp.transpose(eig_tiles[0], (0, 2, 1, 3)).reshape(tile_rows * tile, groups, piece)
    moved = lax.all_to_all(local, "mp", split_axis=1, concat_axis=1, tiled=True)
    moved = moved.reshape(tile_rows, tile, grid_rows, grid_cols, piece)
    basis = jnp.transpose(moved, (0, 2, 1, 3, 4)).reshape(width, slab)
    ordered = jnp.transpose(eigvals.reshape(tile_cols, grid_cols, tile), (1, 0, 2)).reshape(
        grid_cols, groups, piece
    )
    ordered = jnp.transpose(ordered, (1, 0, 2)).reshape(width)
    own = lax.dynamic_slice_in_dim(ordered, member * slab, slab)
    proj_in = jnp.dot(inputs, basis, preferred_element_type=jnp.float32).astype(jnp.bfloat16)
    proj_up = jnp.dot(upstream, basis, preferred_element_type=jnp.float32).astype(jnp.bfloat16)
    stacked = jnp.stack([proj_in, proj_up], 0)
    over_tokens = (((0,), (0,)), ((), ()))
    pieces = lax.all_gather(stacked, "mp", axis=2, tiled=True)
    part_in = pieces[0]
    part_up = pieces[1]
    block = lax.dot_general(proj_in, part_up, over_tokens, preferred_element_type=jnp.float32)
    block = block + lax.dot_general(
        proj_up, part_in, over_tokens, preferred_element_type=jnp.float32
    )
    joined = jnp.concatenate([block, part_in.astype(jnp.float32)], 0)
    gram = joined[:slab]
    all_in = joined[slab:].astype(jnp.bfloat16)
    total = lax.psum(gram.astype(jnp.bfloat16), "dp").astype(jnp.float32)
    weighted = (kernel_of(own, ordered) * (0.5 * total)).astype(jnp.bfloat16)
    over_columns = (((1,), (1,)), ((), ()))
    mixed = lax.dot_general(all_in, weighted, over_columns, preferred_element_type=jnp.float32)
    factor = 2.0 / (lax.axis_size("dp") * inputs.shape[0])
    update = (proj_up.astype(jnp.float32) / jnp.sqrt(own)[None, :] + factor * mixed).astype(
        jnp.bfloat16
    )
    own_rows = lax.all_to_all(basis, "mp", split_axis=0, concat_axis=1, tiled=True)
    every_update = lax.all_gather(update, "mp", axis=1, tiled=True)
    result = lax.dot_general(
        own_rows, every_update, over_columns, preferred_element_type=jnp.float32
    )
    return result.astype(jnp.bfloat16)


def solution(mesh):
    return jax.shard_map(
        on_device,
        mesh=mesh,
        in_specs=(P("dp", None), P("dp", None), P("mp", None, None, None, None), P()),
        out_specs=P("mp", "dp"),
        check_vma=False,
    )
```

profile of v0, /device:TPU:28, one launch (start us, length us, event | category | flops | bytes accessed | tf_op | source)
XLA Modules:
  0.0 280.6 jit_solution(1150355094746853102)
XLA Ops:
  6.5 0.0 copy-start
  6.5 0.0 all-gather.3.cloned.1.call-start
  6.5 4.2 %copy.17 = bf16[8,128,8,128]{1,0,3,2:T(8,128)(2,1)} copy(bf16[8,128,8,128]{3,1,2,0:T(8,128)(2,1)} %bitcast.56) | data formatting | bytes 4194304 | tf_op jit(solution)/shard_map/transpose | solution.py:24
  10.8 4.2 %reshape.29 = bf16[1024,16,64]{0,2,1:T(8,128)(2,1)} reshape(bf16[8,128,8,128]{1,0,3,2:T(8,128)(2,1)} %copy.17) | data formatting | bytes 4194304 | tf_op jit(solution)/shard_map/reshape | solution.py:24
  14.9 53.7 %all_to_all.24 = bf16[1024,16,64]{0,2,1:T(8,128)(2,1)S(1)} all-to-all(bf16[1024,16,64]{0,2,1:T(8,128)(2,1)} %reshape.29), channel_id=1, replica_groups=mesh['dp'=2,'mp'=16] {'mp'}, dimensions={1} | all-to-all | bytes 4194304 | tf_op jit(solution)/shard_map/all_to_all | solution.py:25
  68.6 0.6 copy.23
  69.2 4.0 %copy.25 = bf16[8,128,4,4,64]{1,2,0,4,3:T(4,128)(2,1)} copy(bf16[8,128,4,4,64]{1,0,4,3,2:T(8,128)(2,1)S(1)} %bitcast.55) | data formatting | bytes 4194304 | tf_op jit(solution)/shard_map/reshape | solution.py:26
  73.3 4.5 %reshape.31 = bf16[4096,256]{0,1:T(8,128)(2,1)} reshape(bf16[8,4,128,4,64]{2,1,0,4,3:T(4,128)(2,1)} %bitcast.52) | data formatting | bytes 4194304 | tf_op jit(solution)/shard_map/reshape | solution.py:27
  77.8 0.0 copy-done
  77.8 0.0 copy-start.2
  77.8 0.0 copy-start.4
  77.8 2.5 convolution_convert_fusion.2
  80.2 0.0 copy-done.2
  80.3 0.3 copy-done.4
  80.6 0.7 convolution_convert_fusion.1
  81.4 0.7 pad_maximum_fusion
  82.1 0.0 all-gather.3.cloned.1.call-update
  82.1 0.0 all-reduce.2.cloned.1.call-start
  82.1 84.0 %all-gather.3.cloned.1.call-done = bf16[2,256,4096]{2,1,0:T(8,128)(2,1)} async-done(((bf16[2,256,256]{2,1,0:T(8,128)(2,1)}), bf16[2,256,4096]{2,1,0:T(8,128)(2,1)}) %all-gather.3.cloned.1.call-update) | async-done | bytes 4194320 | tf_op jit(solution)/shard_map/all_gather | solution.py:37
  166.2 0.0 copy-start.1
  166.2 2.5 fusion.1
  168.7 0.3 copy-done.1
  169.0 2.1 fusion
  171.1 0.0 copy-start.3
  171.1 0.0 all-reduce.2.cloned.1.call-update
  171.1 0.7 copy-done.3
  171.8 0.1 reshape.33
  171.9 0.1 reshape.34
  172.0 0.1 dynamic-slice_sqrt_fusion
  172.1 4.4 %all_to_all.18 = bf16[16,256,256]{1,0,2:T(8,128)(2,1)} reshape(bf16[8,4,128,4,64]{2,1,0,4,3:T(4,128)(2,1)} %bitcast.53) | data formatting | bytes 4194304 | tf_op jit(solution)/shard_map/all_to_all | solution.py:55
  176.5 3.6 %copy.21 = bf16[16,256,256]{1,2,0:T(8,128)(2,1)} copy(bf16[16,256,256]{1,0,2:T(8,128)(2,1)} %all_to_all.18) | data formatting | bytes 4194304 | tf_op jit(solution)/shard_map/all_to_all | solution.py:55
  180.1 7.7 %all-to-all-start.1 = ((bf16[16,256,256]{1,2,0:T(8,128)(2,1)}), bf16[16,256,256]{1,2,0:T(8,128)(2,1)}, u32[]{:S(2)}, u32[]{:S(2)}) async-start(bf16[16,256,256]{1,2,0:T(8,128)(2,1)} %copy.21), calls=%async_computation.1 | async-start | bytes 4194304 | tf_op jit(solution)/shard_map/all_to_all | solution.py:55
  187.8 0.0 all-gather.5.cloned.1.call-start
  187.8 6.1 %all-reduce.2.cloned.1.call-done = bf16[256,4096]{1,0:T(8,128)(2,1)} async-done(((bf16[256,4096]{1,0:T(8,128)(2,1)}), bf16[256,4096]{1,0:T(8,128)(2,1)}) %all-reduce.2.cloned.1.call-update) | async-done | bytes 2097168 | tf_op jit(solution)/shard_map/psum | solution.py:47
  193.9 4.4 %fusion.5 = bf16[256,256]{1,0:T(8,128)(2,1)} fusion(bf16[256,4096]{1,0:T(8,128)(2,1)} %all-reduce.2.cloned.1.call-done, f32[4096]{0:T(1024)S(1)} %sqrt.12, f32[256]{0:T(256)S(1)} %dynamic-slice_sqrt_fusion, bf16[2,256,4096]{2,1,0:T(8,128)(2,1)} %all-gather.3.cloned.1.call-done, bf16[256,256]{1,0:T(8,128)(2,1)S(1)} %convolution_convert_fusion.2), kind=kOutput, calls=%fused_computation.10 | convolution fusion | flops 545587200 | bytes 4474880 | tf_op jit(solution)/shard_map/dot_general | solution.py:50
  198.3 0.0 all-gather.5.cloned.1.call-update
  198.3 39.4 %all-to-all-done.1 = bf16[16,256,256]{1,2,0:T(8,128)(2,1)} async-done(((bf16[16,256,256]{1,2,0:T(8,128)(2,1)}), bf16[16,256,256]{1,2,0:T(8,128)(2,1)}, u32[]{:S(2)}, u32[]{:S(2)}) %all-to-all-start.1) | async-done | bytes 2097184 | tf_op jit(solution)/shard_map/all_to_all | solution.py:55
  237.7 32.7 %all-gather.5.cloned.1.call-done = bf16[256,4096]{1,0:T(8,128)(2,1)} async-done(((bf16[256,256]{1,0:T(8,128)(2,1)}), bf16[256,4096]{1,0:T(8,128)(2,1)}) %all-gather.5.cloned.1.call-update) | async-done | bytes 2097168 | tf_op jit(solution)/shard_map/all_gather | solution.py:56
  270.4 2.9 %fusion.6 = bf16[256,256]{0,1:T(8,128)(2,1)S(1)} fusion(bf16[256,4096]{1,0:T(8,128)(2,1)} %all-gather.5.cloned.1.call-done, bf16[256,4096]{0,1:T(8,128)(2,1)} %bitcast.11), kind=kOutput, calls=%fused_computation.14 | convolution fusion | flops 536936448 | bytes 4325376 | tf_op jit(solution)/shard_map/dot_general | solution.py:57
  273.3 0.8 copy.22
  (3 shorter events, 0.0 us)
Async XLA Ops:
  6.5 71.2 %copy-start = (bf16[256,4096]{1,0:T(8,128)(2,1)S(1)}, bf16[256,4096]{1,0:T(8,128)(2,1)}, u32[]{:S(2)}) copy-start(bf16[256,4096]{1,0:T(8,128)(2,1)} %param.5) | copy-start | bytes 6291460
  6.5 159.7 %all-gather.3.cloned.1.call-start = ((), (), s32[]{:S(2)}) async-start(), calls=%async_computation.2 | async-start | bytes 4456448 | tf_op jit(solution)/shard_map/all_gather | solution.py:37
  77.8 2.5 copy-start.2
  77.8 2.9 %copy-start.4 = (bf16[256,4096]{1,0:T(8,128)(2,1)S(1)}, bf16[256,4096]{1,0:T(8,128)(2,1)}, u32[]{:S(2)}) copy-start(bf16[256,4096]{1,0:T(8,128)(2,1)} %param.4) | copy-start | bytes 6291460
  82.1 111.8 %all-reduce.2.cloned.1.call-start = ((), (), s32[]{:S(2)}) async-start(), calls=%async_computation.3 | async-start | bytes 4194304 | tf_op jit(solution)/shard_map/psum | solution.py:47
  166.2 2.8 %copy-start.1 = (bf16[2,256,4096]{2,1,0:T(8,128)(2,1)S(1)}, bf16[2,256,4096]{2,1,0:T(8,128)(2,1)}, u32[]{:S(2)}) copy-start(bf16[2,256,4096]{2,1,0:T(8,128)(2,1)} %all-gather.3.cloned.1.call-done) | copy-start | bytes 12582916
  171.1 0.7 copy-start.3
  180.1 57.6 %all-to-all-start.1 = ((bf16[16,256,256]{1,2,0:T(8,128)(2,1)}), bf16[16,256,256]{1,2,0:T(8,128)(2,1)}, u32[]{:S(2)}, u32[]{:S(2)}) async-start(bf16[16,256,256]{1,2,0:T(8,128)(2,1)} %copy.21), calls=%async_computation.1 | async-start | bytes 4194304 | tf_op jit(solution)/shard_map/all_to_all | solution.py:55
  187.8 82.6 %all-gather.5.cloned.1.call-start = ((), (), s32[]{:S(2)}) async-start(), calls=%async_computation.4 | async-start | bytes 2228224 | tf_op jit(solution)/shard_map/all_gather | solution.py:56
Sparse Core Ops, SparseCore 0:
  82.2 83.9 all-gather.2
  171.3 22.6 all-reduce.1
  198.4 71.9 all-gather.4
where the time goes:
time: 286 us; the launch traced here: 281 us
  waiting for transfers between devices  162 us (57%)
  blocking collectives  53.7 us (19%)
  local copies, waits for them, and re-layouts  28 us (10%)
  matrix products  15.1 us (5%)
  between operations  13.2 us (5%)
  starting transfers between devices  7.74 us (3%)
    all_gather x1, waiting for transfers between devices, on_device(): pieces = lax.all_gather(stacked, 'mp', axis=2, tiled=True)  84 us
    all_to_all x1, blocking collectives, on_device(): moved = lax.all_to_all(local, 'mp', split_axis=1, concat_axis=1, tiled=True)  53.7 us
    all_to_all x1, waiting for transfers between devices, on_device(): lax.all_to_all(basis, 'mp', split_axis=0, concat_axis=1, tiled=True)  39.4 us
    all_gather x1, waiting for transfers between devices, on_device(): every_update = lax.all_gather(update, 'mp', axis=1, tiled=True)  32.7 us
    all_to_all x2, local copies, waits for them, and re-layouts, on_device(): lax.all_to_all(basis, 'mp', split_axis=0, concat_axis=1, tiled=True)  8.02 us
    all_to_all x1, starting transfers between devices, on_device(): lax.all_to_all(basis, 'mp', split_axis=0, concat_axis=1, tiled=True)  7.66 us
    psum x1, waiting for transfers between devices, on_device(): total = lax.psum(gram.astype(jnp.bfloat16), 'dp').astype(jnp.float32)  6.08 us
  transfers between devices with their start and end apart: 4, of which 4 were waited for; matrix products, arithmetic and copies ran while one was open for 3% of the time, Pallas kernels for 0%

commit v1 on v0

--- a/solution.py
+++ b/solution.py
@@ -1,6 +1,10 @@
+import functools
+
 import jax
 import jax.numpy as jnp
 from jax import lax
+from jax.experimental import pallas as pl
+from jax.experimental.pallas import tpu as pltpu
 from jax.sharding import PartitionSpec as P
 
 
@@ -60,9 +64,379 @@
     return result.astype(jnp.bfloat16)
 
 
+def line_kernel(
+    dims, ev, x_in, x_up, eig, out,
+    ub, xb, pf, sup, sdn, rup, rdn, gz, gp, kb, so, ss, sr, mx, ms, mr, uz, ff, fs, fb,
+    ld_u, ld_x, up_s, up_r, dn_s, dn_r, zu_s, zd_s, z_r, p_s, p_r, c_s, c_r,
+    m_s, m_r, wu_s, wd_s, w_r, f_s, f_r,
+):
+    R, C, tr, tc, tile, slab, factor = dims
+    q = slab // tile
+    n = R * C
+    rows = tr * tile
+    d = lax.axis_index("dp")
+    me = lax.axis_index("mp")
+    r = me // C
+    c = me % C
+    partner = (1 - d, me)
+    above = (d, (me + C) % n)
+    below = (d, (me + n - C) % n)
+    f32, bf16 = jnp.float32, jnp.bfloat16
+
+    def remote(src, dst, s_sem, r_sem, dev):
+        return pltpu.make_async_remote_copy(
+            src_ref=src, dst_ref=dst, send_sem=s_sem, recv_sem=r_sem,
+            device_id=dev, device_id_type=pl.DeviceIdType.MESH,
+        )
+
+    def arrived(dst, r_sem):
+        remote(dst, dst, c_s.at[0, 0], r_sem, partner).wait_recv()
+
+    def left(src, s_sem):
+        remote(src, src, s_sem, c_r.at[0, 0], partner).wait_send()
+
+    for h, x in enumerate((x_in, x_up)):
+        for la in range(tr):
+            col = pl.multiple_of((la * R + r) * tile, tile)
+            pltpu.make_async_copy(
+                x.at[:, pl.ds(col, tile)], xb.at[h, :, la * tile:(la + 1) * tile], ld_x.at[h]
+            ).start()
+        if h == 0:
+            for t in [R - 1, 0] + list(range(R - 2, 0, -1)):
+                for k in range(q):
+                    for la in range(tr):
+                        pltpu.make_async_copy(
+                            eig.at[0, la, t * q + k],
+                            ub.at[t, la * tile:(la + 1) * tile, k * tile:(k + 1) * tile],
+                            ld_u.at[t],
+                        ).start()
+    barrier = pltpu.get_barrier_semaphore()
+    for k in range(1, n):
+        pl.semaphore_signal(
+            barrier, inc=1, device_id=(d, (me + k) % n), device_id_type=pl.DeviceIdType.MESH
+        )
+    pl.semaphore_signal(
+        barrier, inc=1, device_id=partner, device_id_type=pl.DeviceIdType.MESH
+    )
+    pl.semaphore_wait(barrier, n)
+
+    for h in range(2):
+        pltpu.make_async_copy(xb.at[h], xb.at[h], ld_x.at[h]).wait()
+        for t in [R - 1, 0] + list(range(R - 2, 0, -1)):
+            if h == 0:
+                pltpu.make_async_copy(ub.at[t], ub.at[t], ld_u.at[t]).wait()
+            pf[h, t] = jnp.dot(xb[h], ub[t], preferred_element_type=f32)
+            if t > 0:
+                @pl.when(r == 0)
+                def _():
+                    sup[h, t] = pf[h, t].astype(bf16)
+                    remote(sup.at[h, t], rup.at[h, t], up_s.at[h, t], up_r.at[h, t], above).start()
+            if t < R - 1:
+                @pl.when(r == R - 1)
+                def _():
+                    sdn[h, t] = pf[h, t].astype(bf16)
+                    remote(sdn.at[h, t], rdn.at[h, t], dn_s.at[h, t], dn_r.at[h, t], below).start()
+
+    def kernel_rows(lb, carry):
+        row = jnp.sqrt(ev[pl.ds(lb * C + c, 1), :])
+        sj = jnp.broadcast_to(row, (tile, tile)).T
+        t = lb // q
+        at = pl.multiple_of((lb % q) * tile, tile)
+        for cc in range(C):
+            for k in range(q):
+                si = jnp.sqrt(ev[pl.ds((r * q + k) * C + cc, 1), :])
+                kb[t, cc, pl.ds(at, tile), k * tile:(k + 1) * tile] = -0.5 / (si * sj * (si + sj))
+        return carry
+
+    lax.fori_loop(0, tc, kernel_rows, 0)
+
+    def relay_up(h):
+        for t in range(R - 1, 0, -1):
+            @pl.when((r > 0) & (r < t))
+            def _():
+                arrived(rup.at[h, t], up_r.at[h, t])
+                sup[h, t] = (pf[h, t] + rup[h, t].astype(f32)).astype(bf16)
+                remote(sup.at[h, t], rup.at[h, t], up_s.at[h, t], up_r.at[h, t], above).start()
+
+    def relay_down(h):
+        for t in range(R - 1):
+            @pl.when((r < R - 1) & (r > t))
+            def _():
+                arrived(rdn.at[h, t], dn_r.at[h, t])
+                sdn[h, t] = (pf[h, t] + rdn[h, t].astype(f32)).astype(bf16)
+                remote(sdn.at[h, t], rdn.at[h, t], dn_s.at[h, t], dn_r.at[h, t], below).start()
+
+    for h in range(2):
+        @pl.when(r < R // 2)
+        def _():
+            relay_up(h)
+            relay_down(h)
+
+        @pl.when(r >= R // 2)
+        def _():
+            relay_down(h)
+            relay_up(h)
+
+        for t in range(R):
+            @pl.when(r == t)
+            def _():
+                total = pf[h, t]
+                if t > 0:
+                    arrived(rup.at[h, t], up_r.at[h, t])
+                    total = total + rup[h, t].astype(f32)
+                if t < R - 1:
+                    arrived(rdn.at[h, t], dn_r.at[h, t])
+                    total = total + rdn[h, t].astype(f32)
+                total = total.astype(bf16)
+                gz[h, t] = total
+                if t < R - 1:
+                    remote(gz.at[h, t], gz.at[h, t], zu_s.at[h, t], z_r.at[h, t], above).start()
+                if t > 0:
+                    remote(gz.at[h, t], gz.at[h, t], zd_s.at[h, t], z_r.at[h, t], below).start()
+                gp[h, c] = total
+        for k in range(1, C):
+            cc = (c + k) % C
+            remote(
+                gp.at[h, c], gp.at[h, c], p_s.at[h, k], p_r.at[h, c], (d, r * C + cc)
+            ).start()
+
+    def each_piece(body):
+        body(r, None)
+        for k in range(1, R):
+            @pl.when(r >= k)
+            def _():
+                body(r - k, True)
+
+            @pl.when(r + k < R)
+            def _():
+                body(r + k, False)
+
+    def relay(buf, s, from_below, s_up, s_dn, r_sem):
+        arrived(buf, r_sem)
+        if from_below:
+            @pl.when(r < R - 1)
+            def _():
+                remote(buf, buf, s_up, r_sem, above).start()
+        else:
+            @pl.when(r > 0)
+            def _():
+                remote(buf, buf, s_dn, r_sem, below).start()
+
+    tokens_both = (((0,), (0,)), ((), ()))
+
+    def gram_piece(s, from_below):
+        if from_below is not None:
+            for h in range(2):
+                relay(
+                    gz.at[h, s], s, from_below, zu_s.at[h, s], zd_s.at[h, s], z_r.at[h, s]
+                )
+
+        def one(cc, carry):
+            block = lax.dot_general(gz[1, s], gp[0, cc], tokens_both, preferred_element_type=f32)
+            block = block + lax.dot_general(
+                gz[0, s], gp[1, cc], tokens_both, preferred_element_type=f32
+            )
+            so[s, cc] = block
+            ss[s, cc] = block.astype(bf16)
+            remote(ss.at[s, cc], sr.at[s, cc], c_s.at[s, cc], c_r.at[s, cc], partner).start()
+            return carry
+
+        lax.fori_loop(0, C, one, 0)
+
+    for h in range(2):
+        for k in range(1, C):
+            cc = (c + k) % C
+            arrived(gp.at[h, cc], p_r.at[h, cc])
+    each_piece(gram_piece)
+
+    mx[...] = jnp.zeros_like(mx)
+
+    def mixed_piece(s, carry):
+        def one(cc, carry):
+            arrived(sr.at[s, cc], c_r.at[s, cc])
+            weighted = (kb[s, cc] * (so[s, cc] + sr[s, cc].astype(f32))).astype(bf16)
+            mx[cc] += jnp.dot(gz[0, s], weighted, preferred_element_type=f32)
+            return carry
+
+        return lax.fori_loop(0, C, one, carry)
+
+    lax.fori_loop(0, R, lambda k, carry: mixed_piece((r + k) % R, carry), 0)
+
+    for k in range(1, C):
+        cc = (c + k) % C
+        ms[cc] = mx[cc].astype(bf16)
+        remote(ms.at[cc], mr.at[c], m_s.at[cc], m_r.at[c], (d, r * C + cc)).start()
+    total = mx[c]
+    for k in range(1, C):
+        cc = (c + k) % C
+        arrived(mr.at[cc], m_r.at[cc])
+        total = total + mr[cc].astype(f32)
+    roots = jnp.concatenate(
+        [jnp.sqrt(ev[pl.ds((r * q + k) * C + c, 1), :]) for k in range(q)], axis=1
+    )
+    uz[r] = (gz[1, r].astype(f32) / roots + factor * total).astype(bf16)
+
+    @pl.when(r < R - 1)
+    def _():
+        remote(uz.at[r], uz.at[r], wu_s.at[r], w_r.at[r], above).start()
+
+    @pl.when(r > 0)
+    def _():
+        remote(uz.at[r], uz.at[r], wd_s.at[r], w_r.at[r], below).start()
+
+    ff[...] = jnp.zeros_like(ff)
+    chunks = rows // slab
+
+    def grad_piece(s, from_below):
+        if from_below is not None:
+            relay(uz.at[s], s, from_below, wu_s.at[s], wd_s.at[s], w_r.at[s])
+
+        def one(i, carry):
+            at = pl.multiple_of(i * slab, slab)
+            ff[i] += lax.dot_general(
+                ub[s, pl.ds(at, slab), :], uz[s], (((1,), (1,)), ((), ())),
+                preferred_element_type=f32,
+            )
+            return carry
+
+        lax.fori_loop(0, chunks, one, 0)
+
+    each_piece(grad_piece)
+
+    for la in range(tr):
+        g = la * R + r
+        owner = g // q
+        pos = g % q
+        part = ff[la // q, (la % q) * tile:(la % q + 1) * tile, :].astype(bf16)
+
+        @pl.when(owner == me)
+        def _():
+            fb[pos, c] = part
+
+        @pl.when(owner != me)
+        def _():
+            fs[la] = part
+            remote(fs.at[la], fb.at[pos, c], f_s.at[la], f_r.at[pos, c], (d, owner)).start()
+
+    for pos in range(q):
+        source = (me * q + pos) % R
+        for cc in range(C):
+            @pl.when((source != r) | (c != cc))
+            def _():
+                arrived(fb.at[pos, cc], f_r.at[pos, cc])
+        total = fb[pos, 0].astype(f32)
+        for cc in range(1, C):
+            total = total + fb[pos, cc].astype(f32)
+        out[pos * tile:(pos + 1) * tile, :] = total.astype(bf16)
+
+    for h in range(2):
+        for t in range(R):
+            if t > 0:
+                @pl.when(r < t)
+                def _():
+                    left(sup.at[h, t], up_s.at[h, t])
+            if t < R - 1:
+                @pl.when(r > t)
+                def _():
+                    left(sdn.at[h, t], dn_s.at[h, t])
+
+            @pl.when((r >= t) & (r < R - 1))
+            def _():
+                left(gz.at[h, t], zu_s.at[h, t])
+
+            @pl.when((r <= t) & (r > 0))
+            def _():
+                left(gz.at[h, t], zd_s.at[h, t])
+        for k in range(1, C):
+            left(gp.at[h, c], p_s.at[h, k])
+    for t in range(R):
+        @pl.when((r >= t) & (r < R - 1))
+        def _():
+            left(uz.at[t], wu_s.at[t])
+
+        @pl.when((r <= t) & (r > 0))
+        def _():
+            left(uz.at[t], wd_s.at[t])
+        for cc in range(C):
+            left(ss.at[t, cc], c_s.at[t, cc])
+    for k in range(1, C):
+        cc = (c + k) % C
+        left(ms.at[cc], m_s.at[cc])
+    for la in range(tr):
+        @pl.when((la * R + r) // q != me)
+        def _():
+            left(fs.at[la], f_s.at[la])
+
+
+def grid_on_device(R, C, inputs, upstream, eig_tiles, eigvals):
+    _, tr, tc, tile, _ = eig_tiles.shape
+    tokens, width = inputs.shape
+    slab = width // (R * C)
+    q = slab // tile
+    rows = tr * tile
+    factor = 2.0 / (lax.axis_size("dp") * tokens)
+    bf16, f32 = jnp.bfloat16, jnp.float32
+    dma = pltpu.SemaphoreType.DMA
+    piece = (tokens, slab)
+    scratch = [
+        pltpu.VMEM((R, rows, slab), bf16),
+        pltpu.VMEM((2, tokens, rows), bf16),
+        pltpu.VMEM((2, R) + piece, f32),
+        pltpu.VMEM((2, R) + piece, bf16),
+        pltpu.VMEM((2, R) + piece, bf16),
+        pltpu.VMEM((2, R) + piece, bf16),
+        pltpu.VMEM((2, R) + piece, bf16),
+        pltpu.VMEM((2, R) + piece, bf16),
+        pltpu.VMEM((2, C) + piece, bf16),
+        pltpu.VMEM((R, C, slab, slab), f32),
+        pltpu.VMEM((R, C, slab, slab), f32),
+        pltpu.VMEM((R, C, slab, slab), bf16),
+        pltpu.VMEM((R, C, slab, slab), bf16),
+        pltpu.VMEM((C,) + piece, f32),
+        pltpu.VMEM((C,) + piece, bf16),
+        pltpu.VMEM((C,) + piece, bf16),
+        pltpu.VMEM((R,) + piece, bf16),
+        pltpu.VMEM((rows // slab, slab, tokens), f32),
+        pltpu.VMEM((tr, tile, tokens), bf16),
+        pltpu.VMEM((q, C, tile, tokens), bf16),
+        dma((R,)), dma((2,)),
+        dma((2, R)), dma((2, R)), dma((2, R)), dma((2, R)),
+        dma((2, R)), dma((2, R)), dma((2, R)),
+        dma((2, C)), dma((2, C)),
+        dma((R, C)), dma((R, C)),
+        dma((C,)), dma((C,)),
+        dma((R,)), dma((R,)), dma((R,)),
+        dma((tr,)), dma((q, C)),
+    ]
+    anywhere = pl.BlockSpec(memory_space=pl.ANY)
+    return pl.pallas_call(
+        functools.partial(line_kernel, (R, C, tr, tc, tile, slab, factor)),
+        out_shape=jax.ShapeDtypeStruct((slab, tokens), bf16),
+        in_specs=[pl.BlockSpec(memory_space=pltpu.VMEM), anywhere, anywhere, anywhere],
+        out_specs=pl.BlockSpec(memory_space=pltpu.VMEM),
+        scratch_shapes=scratch,
+        compiler_params=pltpu.CompilerParams(
+            collective_id=0, has_side_effects=True, vmem_limit_bytes=48 * 2**20
+        ),
+    )(eigvals.reshape(width // tile, tile), inputs, upstream, eig_tiles)
+
+
+def body(inputs, upstream, eig_tiles, eigvals):
+    width = inputs.shape[1]
+    groups = lax.axis_size("mp")
+    _, tr, tc, tile, _ = eig_tiles.shape
+    R = width // (tr * tile)
+    C = groups // R
+    slab = width // groups
+    whole_tiles = slab % tile == 0 and (tr * tile) % slab == 0 and tc % R == 0
+    if lax.axis_size("dp") == 2 and whole_tiles and R > 1 and C > 1:
+        return grid_on_device(R, C, inputs, upstream, eig_tiles, eigvals)
+    return on_device(inputs, upstream, eig_tiles, eigvals)
+
+
 def solution(mesh):
     return jax.shard_map(
-        on_device,
+        body,
         mesh=mesh,
         in_specs=(P("dp", None), P("dp", None), P("mp", None, None, None, None), P()),
         out_specs=P("mp", "dp"),

time: 286 us -> 89 us (0.31); the launches traced: 281 us -> 88.7 us
  waiting for transfers between devices: 162 us -> 0 us
  Pallas kernels: 0 us -> 84.2 us
  blocking collectives: 53.7 us -> 0 us
  local copies, waits for them, and re-layouts: 28 us -> 4.56 us
  matrix products: 15.1 us -> 0 us
  between operations: 13.2 us -> 0.01 us
  starting transfers between devices: 7.74 us -> 0 us
    all_gather x2 -> x0, waiting for transfers between devices: 117 us -> none  [the longest x1 84 us: on_device(): pieces = lax.all_gather(stacked, 'mp', axis=2, tiled=True)]
    pallas_call x0 -> x1, Pallas kernels: none -> 84.2 us  [grid_on_device(): pl.pallas_call(functools.partial(line_kernel, (R, C, tr, tc, tile, slab,...]
    all_to_all x1 -> x0, blocking collectives: 53.7 us -> none  [on_device(): moved = lax.all_to_all(local, 'mp', split_axis=1, concat_axis=1, tiled=True)]
    all_to_all x1 -> x0, waiting for transfers between devices: 39.4 us -> none  [on_device(): lax.all_to_all(basis, 'mp', split_axis=0, concat_axis=1, tiled=True)]
    dot_general x6 -> x0, matrix products: 15.1 us -> none  [the longest x1 4.38 us: on_device(): lax.dot_general(all_in, weighted, over_columns, preferred_element_type=jn...]
    reshape x5 -> x0, local copies, waits for them, and re-layouts: 12.8 us -> none  [the longest x1 4.48 us: on_device(): basis = jnp.transpose(moved, (0, 2, 1, 3, 4)).reshape(width, slab)]
    all_to_all x2 -> x0, local copies, waits for them, and re-layouts: 8.02 us -> none  [on_device(): lax.all_to_all(basis, 'mp', split_axis=0, concat_axis=1, tiled=True)]
    all_to_all x1 -> x0, starting transfers between devices: 7.66 us -> none  [on_device(): lax.all_to_all(basis, 'mp', split_axis=0, concat_axis=1, tiled=True)]
  transfers between devices with their start and end apart: 4 -> 0, of which waited for: 4 -> 0; matrix products, arithmetic and copies ran while one was open for 3% -> 0% of each run, Pallas kernels for 0% -> 0%
where the time goes in v1:
time: 89 us; the launch traced here: 88.7 us
  Pallas kernels  84.2 us (95%)
  local copies, waits for them, and re-layouts  4.56 us (5%)
    pallas_call x1, Pallas kernels, grid_on_device(): pl.pallas_call(functools.partial(line_kernel, (R, C, tr, tc, tile, slab,...  84.2 us
    unnamed x7, local copies, waits for them, and re-layouts  4.56 us

profile of v1, /device:TPU:28, one launch (start us, length us, event | category | flops | bytes accessed | tf_op | source)
XLA Modules:
  0.0 88.7 jit_solution(4072415305157343571)
XLA Ops:
  0.0 0.0 copy-start
  0.0 1.6 %copy-done = bf16[256,4096]{1,0:T(8,128)(2,1)S(1)} copy-done((bf16[256,4096]{1,0:T(8,128)(2,1)S(1)}, bf16[256,4096]{1,0:T(8,128)(2,1)}, u32[]{:S(2)}) %copy-start) | copy-done | bytes 2097176
  1.6 0.0 copy-start.1
  1.6 1.6 %copy-done.1 = bf16[256,4096]{1,0:T(8,128)(2,1)S(1)} copy-done((bf16[256,4096]{1,0:T(8,128)(2,1)S(1)}, bf16[256,4096]{1,0:T(8,128)(2,1)}, u32[]{:S(2)}) %copy-start.1) | copy-done | bytes 2097176
  3.2 0.0 copy-start.2
  3.2 0.7 copy-done.2
  3.9 84.2 %shard_map.46 = bf16[256,256]{1,0:T(8,128)(2,1)S(1)} custom-call(f32[32,128]{1,0:T(8,128)S(1)} %bitcast.1, bf16[256,4096]{1,0:T(8,128)(2,1)S(1)} %copy-done, bf16[256,4096]{1,0:T(8,128)(2,1)S(1)} %copy-done.1, bf16[1,8,8,128,128]{4,3,2,1,0:T(8,128)(2,1)} %eig.1), custom_call_target="tpu_custom_call" | custom-call | tf_op jit(solution)/shard_map/pallas_call | solution.py:412
  88.1 0.7 copy.6
Async XLA Ops:
  0.0 1.6 %copy-start = (bf16[256,4096]{1,0:T(8,128)(2,1)S(1)}, bf16[256,4096]{1,0:T(8,128)(2,1)}, u32[]{:S(2)}) copy-start(bf16[256,4096]{1,0:T(8,128)(2,1)} %x_in.1) | copy-start | bytes 6291460
  1.6 1.6 %copy-start.1 = (bf16[256,4096]{1,0:T(8,128)(2,1)S(1)}, bf16[256,4096]{1,0:T(8,128)(2,1)}, u32[]{:S(2)}) copy-start(bf16[256,4096]{1,0:T(8,128)(2,1)} %x_up.1) | copy-start | bytes 6291460
  3.2 0.7 copy-start.2

commit v2 on v1

--- a/solution.py
+++ b/solution.py
@@ -66,11 +66,11 @@
 
 def line_kernel(
     dims, ev, x_in, x_up, eig, out,
-    ub, xb, pf, sup, sdn, rup, rdn, gz, gp, kb, so, ss, sr, mx, ms, mr, uz, ff, fs, fb,
+    ub, xb, pf, sup, sdn, rup, rdn, gz, gp, kb, so, ss, sr, mx, ms, mr, uz, ff, fs, fa, fc, fb,
     ld_u, ld_x, up_s, up_r, dn_s, dn_r, zu_s, zd_s, z_r, p_s, p_r, c_s, c_r,
-    m_s, m_r, wu_s, wd_s, w_r, f_s, f_r,
+    m_s, m_r, wu_s, wd_s, w_r, f_s, f_r, o_s, o_r,
 ):
-    R, C, tr, tc, tile, slab, factor = dims
+    R, C, tr, tc, tile, slab, tokens, parts, factor = dims
     q = slab // tile
     n = R * C
     rows = tr * tile
@@ -82,6 +82,9 @@
     above = (d, (me + C) % n)
     below = (d, (me + n - C) % n)
     f32, bf16 = jnp.float32, jnp.bfloat16
+
+    def span(i):
+        return pl.ds(i * (tokens // parts), tokens // parts)
 
     def remote(src, dst, s_sem, r_sem, dev):
         return pltpu.make_async_remote_copy(
@@ -189,10 +192,12 @@
                     total = total + rdn[h, t].astype(f32)
                 total = total.astype(bf16)
                 gz[h, t] = total
-                if t < R - 1:
-                    remote(gz.at[h, t], gz.at[h, t], zu_s.at[h, t], z_r.at[h, t], above).start()
-                if t > 0:
-                    remote(gz.at[h, t], gz.at[h, t], zd_s.at[h, t], z_r.at[h, t], below).start()
+                for i in range(parts):
+                    buf = gz.at[h, t, span(i)]
+                    if t < R - 1:
+                        remote(buf, buf, zu_s.at[h, i, t], z_r.at[h, i, t], above).start()
+                    if t > 0:
+                        remote(buf, buf, zd_s.at[h, i, t], z_r.at[h, i, t], below).start()
                 gp[h, c] = total
         for k in range(1, C):
             cc = (c + k) % C
@@ -223,13 +228,22 @@
                 remote(buf, buf, s_dn, r_sem, below).start()
 
     tokens_both = (((0,), (0,)), ((), ()))
+    mx[...] = jnp.zeros_like(mx)
+
+    def mixed_block(s, cc, carry):
+        arrived(sr.at[s, cc], c_r.at[s, cc])
+        weighted = (kb[s, cc] * (so[s, cc] + sr[s, cc].astype(f32))).astype(bf16)
+        mx[cc] += jnp.dot(gz[0, s], weighted, preferred_element_type=f32)
+        return carry
 
     def gram_piece(s, from_below):
         if from_below is not None:
             for h in range(2):
-                relay(
-                    gz.at[h, s], s, from_below, zu_s.at[h, s], zd_s.at[h, s], z_r.at[h, s]
-                )
+                for i in range(parts):
+                    relay(
+                        gz.at[h, s, span(i)], s, from_below,
+                        zu_s.at[h, i, s], zd_s.at[h, i, s], z_r.at[h, i, s],
+                    )
 
         def one(cc, carry):
             block = lax.dot_general(gz[1, s], gp[0, cc], tokens_both, preferred_element_type=f32)
@@ -242,25 +256,13 @@
             return carry
 
         lax.fori_loop(0, C, one, 0)
+        lax.fori_loop(0, C, functools.partial(mixed_block, s), 0)
 
     for h in range(2):
         for k in range(1, C):
             cc = (c + k) % C
             arrived(gp.at[h, cc], p_r.at[h, cc])
     each_piece(gram_piece)
-
-    mx[...] = jnp.zeros_like(mx)
-
-    def mixed_piece(s, carry):
-        def one(cc, carry):
-            arrived(sr.at[s, cc], c_r.at[s, cc])
-            weighted = (kb[s, cc] * (so[s, cc] + sr[s, cc].astype(f32))).astype(bf16)
-            mx[cc] += jnp.dot(gz[0, s], weighted, preferred_element_type=f32)
-            return carry
-
-        return lax.fori_loop(0, C, one, carry)
-
-    lax.fori_loop(0, R, lambda k, carry: mixed_piece((r + k) % R, carry), 0)
 
     for k in range(1, C):
         cc = (c + k) % C
@@ -276,20 +278,26 @@
     )
     uz[r] = (gz[1, r].astype(f32) / roots + factor * total).astype(bf16)
 
-    @pl.when(r < R - 1)
-    def _():
-        remote(uz.at[r], uz.at[r], wu_s.at[r], w_r.at[r], above).start()
-
-    @pl.when(r > 0)
-    def _():
-        remote(uz.at[r], uz.at[r], wd_s.at[r], w_r.at[r], below).start()
+    for i in range(parts):
+        buf = uz.at[r, span(i)]
+
+        @pl.when(r < R - 1)
+        def _():
+            remote(buf, buf, wu_s.at[i, r], w_r.at[i, r], above).start()
+
+        @pl.when(r > 0)
+        def _():
+            remote(buf, buf, wd_s.at[i, r], w_r.at[i, r], below).start()
 
     ff[...] = jnp.zeros_like(ff)
     chunks = rows // slab
 
     def grad_piece(s, from_below):
         if from_below is not None:
-            relay(uz.at[s], s, from_below, wu_s.at[s], wd_s.at[s], w_r.at[s])
+            for i in range(parts):
+                relay(
+                    uz.at[s, span(i)], s, from_below, wu_s.at[i, s], wd_s.at[i, s], w_r.at[i, s]
+                )
 
         def one(i, carry):
             at = pl.multiple_of(i * slab, slab)
@@ -303,31 +311,46 @@
 
     each_piece(grad_piece)
 
+    half = C // 2
     for la in range(tr):
-        g = la * R + r
-        owner = g // q
-        pos = g % q
-        part = ff[la // q, (la % q) * tile:(la % q + 1) * tile, :].astype(bf16)
+        place = (la % 2) * half + (la // 2) % half
+        fs[la] = ff[la // q, (la % q) * tile:(la % q + 1) * tile, :].astype(bf16)
+
+        @pl.when(c != place)
+        def _():
+            remote(
+                fs.at[la], fa.at[la // C, c], f_s.at[la], f_r.at[la // C, c], (d, r * C + place)
+            ).start()
+
+    for j in range(tr // C):
+        la = c // half + 2 * (c % half) + C * j
+        total = fs[la].astype(f32)
+        for k in range(1, C):
+            cc = (c + k) % C
+            arrived(fa.at[j, cc], f_r.at[j, cc])
+            total = total + fa[j, cc].astype(f32)
+        owner = (la * R + r) // q
+        pos = (la * R + r) % q
+        fc[j] = total.astype(bf16)
 
         @pl.when(owner == me)
         def _():
-            fb[pos, c] = part
+            fb[pos] = fc[j]
 
         @pl.when(owner != me)
         def _():
-            fs[la] = part
-            remote(fs.at[la], fb.at[pos, c], f_s.at[la], f_r.at[pos, c], (d, owner)).start()
+            remote(fc.at[j], fb.at[pos], o_s.at[j], o_r.at[pos], (d, owner)).start()
 
     for pos in range(q):
-        source = (me * q + pos) % R
-        for cc in range(C):
-            @pl.when((source != r) | (c != cc))
-            def _():
-                arrived(fb.at[pos, cc], f_r.at[pos, cc])
-        total = fb[pos, 0].astype(f32)
-        for cc in range(1, C):
-            total = total + fb[pos, cc].astype(f32)
-        out[pos * tile:(pos + 1) * tile, :] = total.astype(bf16)
+        g = me * q + pos
+        la = g // R
+        place = (la % 2) * half + (la // 2) % half
+
+        @pl.when((g % R) * C + place != me)
+        def _():
+            arrived(fb.at[pos], o_r.at[pos])
+
+        out[pos * tile:(pos + 1) * tile, :] = fb[pos]
 
     for h in range(2):
         for t in range(R):
@@ -340,32 +363,40 @@
                 def _():
                     left(sdn.at[h, t], dn_s.at[h, t])
 
-            @pl.when((r >= t) & (r < R - 1))
-            def _():
-                left(gz.at[h, t], zu_s.at[h, t])
-
-            @pl.when((r <= t) & (r > 0))
-            def _():
-                left(gz.at[h, t], zd_s.at[h, t])
+            for i in range(parts):
+                @pl.when((r >= t) & (r < R - 1))
+                def _():
+                    left(gz.at[h, t, span(i)], zu_s.at[h, i, t])
+
+                @pl.when((r <= t) & (r > 0))
+                def _():
+                    left(gz.at[h, t, span(i)], zd_s.at[h, i, t])
         for k in range(1, C):
             left(gp.at[h, c], p_s.at[h, k])
     for t in range(R):
-        @pl.when((r >= t) & (r < R - 1))
-        def _():
-            left(uz.at[t], wu_s.at[t])
-
-        @pl.when((r <= t) & (r > 0))
-        def _():
-            left(uz.at[t], wd_s.at[t])
+        for i in range(parts):
+            @pl.when((r >= t) & (r < R - 1))
+            def _():
+                left(uz.at[t, span(i)], wu_s.at[i, t])
+
+            @pl.when((r <= t) & (r > 0))
+            def _():
+                left(uz.at[t, span(i)], wd_s.at[i, t])
         for cc in range(C):
             left(ss.at[t, cc], c_s.at[t, cc])
     for k in range(1, C):
         cc = (c + k) % C
         left(ms.at[cc], m_s.at[cc])
     for la in range(tr):
+        @pl.when(c != (la % 2) * half + (la // 2) % half)
+        def _():
+            left(fs.at[la], f_s.at[la])
+    for j in range(tr // C):
+        la = c // half + 2 * (c % half) + C * j
+
         @pl.when((la * R + r) // q != me)
         def _():
-            left(fs.at[la], f_s.at[la])
+            left(fc.at[j], o_s.at[j])
 
 
 def grid_on_device(R, C, inputs, upstream, eig_tiles, eigvals):
@@ -373,6 +404,7 @@
     tokens, width = inputs.shape
     slab = width // (R * C)
     q = slab // tile
+    parts = 2 if tokens % 32 == 0 else 1
     rows = tr * tile
     factor = 2.0 / (lax.axis_size("dp") * tokens)
     bf16, f32 = jnp.bfloat16, jnp.float32
@@ -398,25 +430,27 @@
         pltpu.VMEM((R,) + piece, bf16),
         pltpu.VMEM((rows // slab, slab, tokens), f32),
         pltpu.VMEM((tr, tile, tokens), bf16),
-        pltpu.VMEM((q, C, tile, tokens), bf16),
+        pltpu.VMEM((tr // C, C, tile, tokens), bf16),
+        pltpu.VMEM((tr // C, tile, tokens), bf16),
+        pltpu.VMEM((q, tile, tokens), bf16),
         dma((R,)), dma((2,)),
         dma((2, R)), dma((2, R)), dma((2, R)), dma((2, R)),
-        dma((2, R)), dma((2, R)), dma((2, R)),
+        dma((2, parts, R)), dma((2, parts, R)), dma((2, parts, R)),
         dma((2, C)), dma((2, C)),
         dma((R, C)), dma((R, C)),
         dma((C,)), dma((C,)),
-        dma((R,)), dma((R,)), dma((R,)),
-        dma((tr,)), dma((q, C)),
+        dma((parts, R)), dma((parts, R)), dma((parts, R)),
+        dma((tr,)), dma((tr // C, C)), dma((tr // C,)), dma((q,)),
     ]
-    anywhere = pl.BlockSpec(memory_space=pl.ANY)
+    anywhere = pl.BlockSpec(memory_space=pltpu.HBM)
     return pl.pallas_call(
-        functools.partial(line_kernel, (R, C, tr, tc, tile, slab, factor)),
+        functools.partial(line_kernel, (R, C, tr, tc, tile, slab, tokens, parts, factor)),
         out_shape=jax.ShapeDtypeStruct((slab, tokens), bf16),
         in_specs=[pl.BlockSpec(memory_space=pltpu.VMEM), anywhere, anywhere, anywhere],
         out_specs=pl.BlockSpec(memory_space=pltpu.VMEM),
         scratch_shapes=scratch,
         compiler_params=pltpu.CompilerParams(
-            collective_id=0, has_side_effects=True, vmem_limit_bytes=48 * 2**20
+            collective_id=0, has_side_effects=True, vmem_limit_bytes=67_043_328
         ),
     )(eigvals.reshape(width // tile, tile), inputs, upstream, eig_tiles)
 
@@ -429,7 +463,7 @@
     C = groups // R
     slab = width // groups
     whole_tiles = slab % tile == 0 and (tr * tile) % slab == 0 and tc % R == 0
-    if lax.axis_size("dp") == 2 and whole_tiles and R > 1 and C > 1:
+    if lax.axis_size("dp") == 2 and whole_tiles and R > 1 and C % 2 == 0 and tr % C == 0:
         return grid_on_device(R, C, inputs, upstream, eig_tiles, eigvals)
     return on_device(inputs, upstream, eig_tiles, eigvals)
 

time: 89 us -> 93.9 us (1.055)
  Pallas kernels: 84.2 us -> 92.2 us
  local copies, waits for them, and re-layouts: 4.56 us -> 1.57 us
    pallas_call x1, Pallas kernels: 84.2 us -> 92.2 us  [grid_on_device(): pl.pallas_call(functools.partial(line_kernel, (R, C, tr, tc, tile, slab,...]
    unnamed x7 -> x1, local copies, waits for them, and re-layouts: 4.56 us -> 1.57 us
where the time goes in v2:
time: 93.9 us; the launch traced here: 93.7 us
  Pallas kernels  92.2 us (98%)
  local copies, waits for them, and re-layouts  1.57 us (2%)
    pallas_call x1, Pallas kernels, grid_on_device(): pl.pallas_call(functools.partial(line_kernel, (R, C, tr, tc, tile, slab,...  92.2 us

profile of v2, /device:TPU:28, one launch (start us, length us, event | category | flops | bytes accessed | tf_op | source)
XLA Modules:
  0.0 93.7 jit_solution(16578286802983083559)
XLA Ops:
  0.0 92.2 %shard_map.46 = bf16[256,256]{1,0:T(8,128)(2,1)} custom-call(f32[32,128]{1,0:T(8,128)} %bitcast.1, bf16[256,4096]{1,0:T(8,128)(2,1)} %x_in.1, bf16[256,4096]{1,0:T(8,128)(2,1)} %x_up.1, bf16[1,8,8,128,128]{4,3,2,1,0:T(8,128)(2,1)} %eig.1), custom_call_target="tpu_custom_call" | custom-call | tf_op jit(solution)/shard_map/pallas_call | solution.py:446
  92.2 1.6 %copy.6 = bf16[256,256]{1,0:T(8,128)(2,1)} copy(bf16[256,256]{1,0:T(8,128)(2,1)} %shard_map.46) | data formatting | bytes 262144

commit v3 on v2

--- a/solution.py
+++ b/solution.py
@@ -66,7 +66,7 @@
 
 def line_kernel(
     dims, ev, x_in, x_up, eig, out,
-    ub, xb, pf, sup, sdn, rup, rdn, gz, gp, kb, so, ss, sr, mx, ms, mr, uz, ff, fs, fa, fc, fb,
+    ub, xb, pf, sup, sdn, rup, rdn, gz, gp, kb, so, ss, sr, zt, mx, ms, mr, uz, ff, fs, fa, fc, fb,
     ld_u, ld_x, up_s, up_r, dn_s, dn_r, zu_s, zd_s, z_r, p_s, p_r, c_s, c_r,
     m_s, m_r, wu_s, wd_s, w_r, f_s, f_r, o_s, o_r,
 ):
@@ -98,6 +98,15 @@
     def left(src, s_sem):
         remote(src, src, s_sem, c_r.at[0, 0], partner).wait_send()
 
+    barrier = pltpu.get_barrier_semaphore()
+    for k in range(1, n):
+        pl.semaphore_signal(
+            barrier, inc=1, device_id=(d, (me + k) % n), device_id_type=pl.DeviceIdType.MESH
+        )
+    pl.semaphore_signal(
+        barrier, inc=1, device_id=partner, device_id_type=pl.DeviceIdType.MESH
+    )
+    order = [R - 1, 0] + list(range(R - 2, 0, -1))
     for h, x in enumerate((x_in, x_up)):
         for la in range(tr):
             col = pl.multiple_of((la * R + r) * tile, tile)
@@ -105,30 +114,24 @@
                 x.at[:, pl.ds(col, tile)], xb.at[h, :, la * tile:(la + 1) * tile], ld_x.at[h]
             ).start()
         if h == 0:
-            for t in [R - 1, 0] + list(range(R - 2, 0, -1)):
+            for t in order:
                 for k in range(q):
-                    for la in range(tr):
-                        pltpu.make_async_copy(
-                            eig.at[0, la, t * q + k],
-                            ub.at[t, la * tile:(la + 1) * tile, k * tile:(k + 1) * tile],
-                            ld_u.at[t],
-                        ).start()
-    barrier = pltpu.get_barrier_semaphore()
-    for k in range(1, n):
-        pl.semaphore_signal(
-            barrier, inc=1, device_id=(d, (me + k) % n), device_id_type=pl.DeviceIdType.MESH
-        )
-    pl.semaphore_signal(
-        barrier, inc=1, device_id=partner, device_id_type=pl.DeviceIdType.MESH
-    )
-    pl.semaphore_wait(barrier, n)
+                    pltpu.make_async_copy(
+                        eig.at[0, :, t * q + k],
+                        ub.at[t, :, :, k * tile:(k + 1) * tile],
+                        ld_u.at[t],
+                    ).start()
 
     for h in range(2):
         pltpu.make_async_copy(xb.at[h], xb.at[h], ld_x.at[h]).wait()
-        for t in [R - 1, 0] + list(range(R - 2, 0, -1)):
+        for t in order:
             if h == 0:
                 pltpu.make_async_copy(ub.at[t], ub.at[t], ld_u.at[t]).wait()
-            pf[h, t] = jnp.dot(xb[h], ub[t], preferred_element_type=f32)
+            pf[h, t] = jnp.dot(
+                xb[h], ub[t].reshape(rows, slab), preferred_element_type=f32
+            )
+            if h == 0 and t == order[0]:
+                pl.semaphore_wait(barrier, n)
             if t > 0:
                 @pl.when(r == 0)
                 def _():
@@ -139,19 +142,6 @@
                 def _():
                     sdn[h, t] = pf[h, t].astype(bf16)
                     remote(sdn.at[h, t], rdn.at[h, t], dn_s.at[h, t], dn_r.at[h, t], below).start()
-
-    def kernel_rows(lb, carry):
-        row = jnp.sqrt(ev[pl.ds(lb * C + c, 1), :])
-        sj = jnp.broadcast_to(row, (tile, tile)).T
-        t = lb // q
-        at = pl.multiple_of((lb % q) * tile, tile)
-        for cc in range(C):
-            for k in range(q):
-                si = jnp.sqrt(ev[pl.ds((r * q + k) * C + cc, 1), :])
-                kb[t, cc, pl.ds(at, tile), k * tile:(k + 1) * tile] = -0.5 / (si * sj * (si + sj))
-        return carry
-
-    lax.fori_loop(0, tc, kernel_rows, 0)
 
     def relay_up(h):
         for t in range(R - 1, 0, -1):
@@ -205,9 +195,23 @@
                 gp.at[h, c], gp.at[h, c], p_s.at[h, k], p_r.at[h, c], (d, r * C + cc)
             ).start()
 
-    def each_piece(body):
-        body(r, None)
-        for k in range(1, R):
+    def kernel_rows(lb, carry):
+        row = jnp.sqrt(ev[pl.ds(lb * C + c, 1), :])
+        sj = jnp.broadcast_to(row, (tile, tile)).T
+        t = lb // q
+        at = pl.multiple_of((lb % q) * tile, tile)
+        for cc in range(C):
+            for k in range(q):
+                si = jnp.sqrt(ev[pl.ds((r * q + k) * C + cc, 1), :])
+                kb[t, cc, pl.ds(at, tile), k * tile:(k + 1) * tile] = -0.5 / (si * sj * (si + sj))
+        return carry
+
+    lax.fori_loop(0, tc, kernel_rows, 0)
+
+    def level(k, body):
+        if k == 0:
+            body(r, None)
+        elif k < R:
             @pl.when(r >= k)
             def _():
                 body(r - k, True)
@@ -227,7 +231,6 @@
             def _():
                 remote(buf, buf, s_dn, r_sem, below).start()
 
-    tokens_both = (((0,), (0,)), ((), ()))
     mx[...] = jnp.zeros_like(mx)
 
     def mixed_block(s, cc, carry):
@@ -236,49 +239,62 @@
         mx[cc] += jnp.dot(gz[0, s], weighted, preferred_element_type=f32)
         return carry
 
+    def relay_piece(s, from_below):
+        for h in range(2):
+            for i in range(parts):
+                relay(
+                    gz.at[h, s, span(i)], s, from_below,
+                    zu_s.at[h, i, s], zd_s.at[h, i, s], z_r.at[h, i, s],
+                )
+
     def gram_piece(s, from_below):
-        if from_below is not None:
-            for h in range(2):
-                for i in range(parts):
-                    relay(
-                        gz.at[h, s, span(i)], s, from_below,
-                        zu_s.at[h, i, s], zd_s.at[h, i, s], z_r.at[h, i, s],
-                    )
+        for h in range(2):
+            zt[h] = gz[h, s].T
 
         def one(cc, carry):
-            block = lax.dot_general(gz[1, s], gp[0, cc], tokens_both, preferred_element_type=f32)
-            block = block + lax.dot_general(
-                gz[0, s], gp[1, cc], tokens_both, preferred_element_type=f32
-            )
+            block = jnp.dot(zt[1], gp[0, cc], preferred_element_type=f32)
+            block = block + jnp.dot(zt[0], gp[1, cc], preferred_element_type=f32)
             so[s, cc] = block
             ss[s, cc] = block.astype(bf16)
             remote(ss.at[s, cc], sr.at[s, cc], c_s.at[s, cc], c_r.at[s, cc], partner).start()
             return carry
 
         lax.fori_loop(0, C, one, 0)
+
+    def mixed_piece(s, from_below):
         lax.fori_loop(0, C, functools.partial(mixed_block, s), 0)
 
+    level(1, relay_piece)
     for h in range(2):
         for k in range(1, C):
             cc = (c + k) % C
             arrived(gp.at[h, cc], p_r.at[h, cc])
-    each_piece(gram_piece)
-
-    for k in range(1, C):
-        cc = (c + k) % C
-        ms[cc] = mx[cc].astype(bf16)
-        remote(ms.at[cc], mr.at[c], m_s.at[cc], m_r.at[c], (d, r * C + cc)).start()
-    total = mx[c]
-    for k in range(1, C):
-        cc = (c + k) % C
-        arrived(mr.at[cc], m_r.at[cc])
-        total = total + mr[cc].astype(f32)
+    for k in range(R):
+        level(k, gram_piece)
+        if k + 2 < R:
+            level(k + 2, relay_piece)
+        if k > 0:
+            level(k - 1, mixed_piece)
+    level(R - 1, mixed_piece)
+
+    for i in range(parts):
+        for k in range(1, C):
+            cc = (c + k) % C
+            ms[cc, span(i)] = mx[cc, span(i)].astype(bf16)
+            remote(
+                ms.at[cc, span(i)], mr.at[c, span(i)], m_s.at[i, cc], m_r.at[i, c],
+                (d, r * C + cc),
+            ).start()
     roots = jnp.concatenate(
         [jnp.sqrt(ev[pl.ds((r * q + k) * C + c, 1), :]) for k in range(q)], axis=1
     )
-    uz[r] = (gz[1, r].astype(f32) / roots + factor * total).astype(bf16)
-
     for i in range(parts):
+        total = mx[c, span(i)]
+        for k in range(1, C):
+            cc = (c + k) % C
+            arrived(mr.at[cc, span(i)], m_r.at[i, cc])
+            total = total + mr[cc, span(i)].astype(f32)
+        uz[r, span(i)] = (gz[1, r, span(i)].astype(f32) / roots + factor * total).astype(bf16)
         buf = uz.at[r, span(i)]
 
         @pl.when(r < R - 1)
@@ -292,24 +308,27 @@
     ff[...] = jnp.zeros_like(ff)
     chunks = rows // slab
 
+    def relay_update(s, from_below):
+        for i in range(parts):
+            relay(
+                uz.at[s, span(i)], s, from_below, wu_s.at[i, s], wd_s.at[i, s], w_r.at[i, s]
+            )
+
     def grad_piece(s, from_below):
-        if from_below is not None:
-            for i in range(parts):
-                relay(
-                    uz.at[s, span(i)], s, from_below, wu_s.at[i, s], wd_s.at[i, s], w_r.at[i, s]
-                )
-
         def one(i, carry):
-            at = pl.multiple_of(i * slab, slab)
             ff[i] += lax.dot_general(
-                ub[s, pl.ds(at, slab), :], uz[s], (((1,), (1,)), ((), ())),
+                ub[s, pl.ds(i * q, q)].reshape(slab, slab), uz[s], (((1,), (1,)), ((), ())),
                 preferred_element_type=f32,
             )
             return carry
 
         lax.fori_loop(0, chunks, one, 0)
 
-    each_piece(grad_piece)
+    for k in range(R):
+        level(k, grad_piece)
+        if k == 0:
+            level(1, relay_update)
+        level(k + 2, relay_update)
 
     half = C // 2
     for la in range(tr):
@@ -386,7 +405,8 @@
             left(ss.at[t, cc], c_s.at[t, cc])
     for k in range(1, C):
         cc = (c + k) % C
-        left(ms.at[cc], m_s.at[cc])
+        for i in range(parts):
+            left(ms.at[cc, span(i)], m_s.at[i, cc])
     for la in range(tr):
         @pl.when(c != (la % 2) * half + (la // 2) % half)
         def _():
@@ -411,7 +431,7 @@
     dma = pltpu.SemaphoreType.DMA
     piece = (tokens, slab)
     scratch = [
-        pltpu.VMEM((R, rows, slab), bf16),
+        pltpu.VMEM((R, tr, tile, slab), bf16),
         pltpu.VMEM((2, tokens, rows), bf16),
         pltpu.VMEM((2, R) + piece, f32),
         pltpu.VMEM((2, R) + piece, bf16),
@@ -424,6 +444,7 @@
         pltpu.VMEM((R, C, slab, slab), f32),
         pltpu.VMEM((R, C, slab, slab), bf16),
         pltpu.VMEM((R, C, slab, slab), bf16),
+        pltpu.VMEM((2, slab, tokens), bf16),
         pltpu.VMEM((C,) + piece, f32),
         pltpu.VMEM((C,) + piece, bf16),
         pltpu.VMEM((C,) + piece, bf16),
@@ -438,7 +459,7 @@
         dma((2, parts, R)), dma((2, parts, R)), dma((2, parts, R)),
         dma((2, C)), dma((2, C)),
         dma((R, C)), dma((R, C)),
-        dma((C,)), dma((C,)),
+        dma((parts, C)), dma((parts, C)),
         dma((parts, R)), dma((parts, R)), dma((parts, R)),
         dma((tr,)), dma((tr // C, C)), dma((tr // C,)), dma((q,)),
     ]
@@ -450,7 +471,7 @@
         out_specs=pl.BlockSpec(memory_space=pltpu.VMEM),
         scratch_shapes=scratch,
         compiler_params=pltpu.CompilerParams(
-            collective_id=0, has_side_effects=True, vmem_limit_bytes=67_043_328
+            collective_id=0, has_side_effects=True, vmem_limit_bytes=65_800_000
         ),
     )(eigvals.reshape(width // tile, tile), inputs, upstream, eig_tiles)
 

time: 93.9 us -> 85.5 us (0.911)
  Pallas kernels: 92.2 us -> 83.4 us
    pallas_call x1, Pallas kernels: 92.2 us -> 83.4 us  [grid_on_device(): pl.pallas_call(functools.partial(line_kernel, (R, C, tr, tc, tile, slab,...]
where the time goes in v3:
time: 85.5 us; the launch traced here: 85 us
  Pallas kernels  83.4 us (98%)
  local copies, waits for them, and re-layouts  1.57 us (2%)
    pallas_call x1, Pallas kernels, grid_on_device(): pl.pallas_call(functools.partial(line_kernel, (R, C, tr, tc, tile, slab,...  83.4 us

profile of v3, /device:TPU:28, one launch (start us, length us, event | category | flops | bytes accessed | tf_op | source)
XLA Modules:
  0.0 85.0 jit_solution(2195725455160029053)
XLA Ops:
  0.0 83.4 %shard_map.46 = bf16[256,256]{1,0:T(8,128)(2,1)} custom-call(f32[32,128]{1,0:T(8,128)} %bitcast.1, bf16[256,4096]{1,0:T(8,128)(2,1)} %x_in.1, bf16[256,4096]{1,0:T(8,128)(2,1)} %x_up.1, bf16[1,8,8,128,128]{4,3,2,1,0:T(8,128)(2,1)} %eig.1), custom_call_target="tpu_custom_call" | custom-call | tf_op jit(solution)/shard_map/pallas_call | solution.py:467
  83.4 1.6 %copy.6 = bf16[256,256]{1,0:T(8,128)(2,1)} copy(bf16[256,256]{1,0:T(8,128)(2,1)} %shard_map.46) | data formatting | bytes 262144

commit v4 on v3

--- a/solution.py
+++ b/solution.py
@@ -264,18 +264,29 @@
     def mixed_piece(s, from_below):
         lax.fori_loop(0, C, functools.partial(mixed_block, s), 0)
 
-    level(1, relay_piece)
+    between = (r > 0) & (r < R - 1)
+
+    def relay_first(k, body):
+        @pl.when(between)
+        def _():
+            level(k, body)
+
+    def relay_last(k, body):
+        @pl.when((r == 0) | (r == R - 1))
+        def _():
+            level(k, body)
+
+    relay_first(1, relay_piece)
     for h in range(2):
         for k in range(1, C):
             cc = (c + k) % C
             arrived(gp.at[h, cc], p_r.at[h, cc])
     for k in range(R):
+        if k > 0:
+            relay_first(k + 1, relay_piece)
         level(k, gram_piece)
-        if k + 2 < R:
-            level(k + 2, relay_piece)
-        if k > 0:
-            level(k - 1, mixed_piece)
-    level(R - 1, mixed_piece)
+        level(k, mixed_piece)
+        relay_last(k + 1, relay_piece)
 
     for i in range(parts):
         for k in range(1, C):
@@ -325,10 +336,12 @@
         lax.fori_loop(0, chunks, one, 0)
 
     for k in range(R):
+        if k > 0:
+            relay_first(k + 1, relay_update)
         level(k, grad_piece)
         if k == 0:
-            level(1, relay_update)
-        level(k + 2, relay_update)
+            relay_first(1, relay_update)
+        relay_last(k + 1, relay_update)
 
     half = C // 2
     for la in range(tr):
@@ -424,7 +437,7 @@
     tokens, width = inputs.shape
     slab = width // (R * C)
     q = slab // tile
-    parts = 2 if tokens % 32 == 0 else 1
+    parts = 4 if tokens % 64 == 0 else 1
     rows = tr * tile
     factor = 2.0 / (lax.axis_size("dp") * tokens)
     bf16, f32 = jnp.bfloat16, jnp.float32

time: 85.5 us -> 84.1 us (0.984)
  Pallas kernels: 83.4 us -> 82.3 us
    pallas_call x1, Pallas kernels: 83.4 us -> 82.3 us  [grid_on_device(): pl.pallas_call(functools.partial(line_kernel, (R, C, tr, tc, tile, slab,...]
where the time goes in v4:
time: 84.1 us; the launch traced here: 83.9 us
  Pallas kernels  82.3 us (98%)
  local copies, waits for them, and re-layouts  1.57 us (2%)
    pallas_call x1, Pallas kernels, grid_on_device(): pl.pallas_call(functools.partial(line_kernel, (R, C, tr, tc, tile, slab,...  82.3 us

profile of v4, /device:TPU:28, one launch (start us, length us, event | category | flops | bytes accessed | tf_op | source)
XLA Modules:
  0.0 83.9 jit_solution(16068148547098644177)
XLA Ops:
  0.0 82.3 %shard_map.46 = bf16[256,256]{1,0:T(8,128)(2,1)} custom-call(f32[32,128]{1,0:T(8,128)} %bitcast.1, bf16[256,4096]{1,0:T(8,128)(2,1)} %x_in.1, bf16[256,4096]{1,0:T(8,128)(2,1)} %x_up.1, bf16[1,8,8,128,128]{4,3,2,1,0:T(8,128)(2,1)} %eig.1), custom_call_target="tpu_custom_call" | custom-call | tf_op jit(solution)/shard_map/pallas_call | solution.py:480
  82.3 1.6 %copy.6 = bf16[256,256]{1,0:T(8,128)(2,1)} copy(bf16[256,256]{1,0:T(8,128)(2,1)} %shard_map.46) | data formatting | bytes 262144

commit v5 on v4

--- a/solution.py
+++ b/solution.py
@@ -206,7 +206,7 @@
                 kb[t, cc, pl.ds(at, tile), k * tile:(k + 1) * tile] = -0.5 / (si * sj * (si + sj))
         return carry
 
-    lax.fori_loop(0, tc, kernel_rows, 0)
+    lax.fori_loop(0, tc, kernel_rows, 0, unroll=2)
 
     def level(k, body):
         if k == 0:
@@ -259,10 +259,10 @@
             remote(ss.at[s, cc], sr.at[s, cc], c_s.at[s, cc], c_r.at[s, cc], partner).start()
             return carry
 
-        lax.fori_loop(0, C, one, 0)
+        lax.fori_loop(0, C, one, 0, unroll=True)
 
     def mixed_piece(s, from_below):
-        lax.fori_loop(0, C, functools.partial(mixed_block, s), 0)
+        lax.fori_loop(0, C, functools.partial(mixed_block, s), 0, unroll=True)
 
     between = (r > 0) & (r < R - 1)
 
@@ -333,7 +333,7 @@
             )
             return carry
 
-        lax.fori_loop(0, chunks, one, 0)
+        lax.fori_loop(0, chunks, one, 0, unroll=True)
 
     for k in range(R):
         if k > 0:

time: 84.1 us -> 83.8 us (level)
  no operation moved by 1% of the time
where the time goes in v5:
time: 83.8 us; the launch traced here: 83.6 us
  Pallas kernels  82 us (98%)
  local copies, waits for them, and re-layouts  1.57 us (2%)
    pallas_call x1, Pallas kernels, grid_on_device(): pl.pallas_call(functools.partial(line_kernel, (R, C, tr, tc, tile, slab,...  82 us

profile of v5, /device:TPU:28, one launch (start us, length us, event | category | flops | bytes accessed | tf_op | source)
XLA Modules:
  0.0 83.6 jit_solution(7872573635792693403)
XLA Ops:
  0.0 82.0 %shard_map.46 = bf16[256,256]{1,0:T(8,128)(2,1)} custom-call(f32[32,128]{1,0:T(8,128)} %bitcast.1, bf16[256,4096]{1,0:T(8,128)(2,1)} %x_in.1, bf16[256,4096]{1,0:T(8,128)(2,1)} %x_up.1, bf16[1,8,8,128,128]{4,3,2,1,0:T(8,128)(2,1)} %eig.1), custom_call_target="tpu_custom_call" | custom-call | tf_op jit(solution)/shard_map/pallas_call | solution.py:480
  82.0 1.6 %copy.6 = bf16[256,256]{1,0:T(8,128)(2,1)} copy(bf16[256,256]{1,0:T(8,128)(2,1)} %shard_map.46) | data formatting | bytes 262144
